TPU v7x, 512 devices: a whole 4x4x16 slice. The times are simulated.
512 devices in a mesh: row: 16 (over z), col: 16 (over y, x_lo, core), depth: 2 (over x_hi).
Axes of the slice: x: 4 (x_hi: 2, x_lo: 2; x = x_hi * 2 + x_lo), y: 4, z: 16, core: 2. Of those that a mesh axis runs over, the one named last changes fastest.
Arguments:
- amplitudes: float32 [3072, 11520], P('row', ('col', 'depth')), may hold values from -6 to 6
- integrals: float32 [11520, 5760], P(('row', 'depth'), 'col'), may hold values from -0.0546875 to 0.0546875
Outputs:
- ladder: float32 [3072, 5760], P(('row', 'depth'), 'col')
All inputs are finite; a program needn't handle non-finite values.
Results may differ from a plain program's by a relative error of at most 0.00007.
Values sent between devices are 32-bit elements; how exact they have to be, the bound alone decides.
No kernel may reach another device: no remote copies, remote signals or barrier semaphores. Data moves between devices by JAX's collectives and lax.ppermute only.
A program may use at most 64 MiB of HBM per device.

v0:
```python
import jax
import jax.numpy as jnp
from jax import lax
from jax.sharding import PartitionSpec as P


def local(amplitudes, integrals):
    slab = lax.all_gather(integrals, "row", axis=0, tiled=True)
    total = jnp.dot(
        lax.all_gather(amplitudes, "col", axis=1, tiled=True),
        slab,
        precision=lax.Precision.HIGHEST,
        preferred_element_type=jnp.float32,
    )
    return lax.psum_scatter(0.5 * total, "depth", scatter_dimension=0, tiled=True)


def solution(mesh):
    placed = (P("row", ("col", "depth")), P(("row", "depth"), "col"))
    return jax.shard_map(
        local, mesh=mesh, in_specs=placed, out_specs=P(("row", "depth"), "col"), check_vma=False
    )
```

profile of v0, /device:TPU:1, one launch (start us, length us, event | category | flops | bytes accessed | tf_op | source)
XLA Modules:
  0.0 213.8 jit_solution(3228303676502207377)
XLA Ops:
  6.5 0.0 all-gather.6.cloned.1.call-start
  6.5 0.7 all-gather.6.cloned.1.call-update
  7.3 0.0 all-gather.4.cloned.1.call-start
  7.3 0.7 all-gather.4.cloned.1.call-update
  8.0 0.0 reduce-scatter.2.cloned.1.call-start
  8.1 53.4 %all-gather.6.cloned.1.call-done = f32[16,360,192]{1,2,0:T(8,128)} async-done(((f32[1,360,192]{1,2,0:T(8,128)}), f32[16,360,192]{1,2,0:T(8,128)}) %all-gather.6.cloned.1.call-update) | async-done | bytes 4423696 | tf_op jit(solution)/shard_map/all_gather | solution.py:10
  61.5 7.2 %copy.4 = f32[16,360,192]{1,0,2:T(8,128)} copy(f32[16,360,192]{1,2,0:T(8,128)} %all-gather.6.cloned.1.call-done) | data formatting | bytes 8847360 | tf_op jit(solution)/shard_map/all_gather | solution.py:10
  68.7 5.9 %reshape.1 = f32[5760,192]{0,1:T(8,128)} reshape(f32[16,360,192]{1,0,2:T(8,128)} %copy.4) | data formatting | bytes 8847360
  74.5 99.1 %all-gather.4.cloned.1.call-done = f32[5760,360]{1,0:T(8,128)} async-done(((f32[360,360]{1,0:T(8,128)}), f32[5760,360]{1,0:T(8,128)}) %all-gather.4.cloned.1.call-update) | async-done | bytes 8294416 | tf_op jit(solution)/shard_map/all_gather | solution.py:8
  173.6 11.8 %convolution_multiply_fusion = f32[192,360]{1,0:T(8,128)} fusion(f32[5760,192]{0,1:T(8,128)} %reshape.1, f32[5760,360]{1,0:T(8,128)} %all-gather.4.cloned.1.call-done), kind=kOutput, calls=%fused_computation | convolution fusion | flops 4777643520 | bytes 12994560 | tf_op jit(solution)/shard_map/dot_general | solution.py:9
  185.4 0.0 reduce-scatter.2.cloned.1.call-update
  185.5 21.8 %reduce-scatter.2.cloned.1.call-done = f32[96,360]{1,0:T(8,128)} async-done(((f32[192,360]{1,0:T(8,128)}), f32[96,360]{1,0:T(8,128)}) %reduce-scatter.2.cloned.1.call-update) | async-done | bytes 138256 | tf_op jit(solution)/shard_map/reduce_scatter | solution.py:15
Async XLA Ops:
  6.5 54.9 %all-gather.6.cloned.1.call-start = ((), (), s32[]{:S(2)}) async-start(), calls=%async_computation.3 | async-start | bytes 5013504 | tf_op jit(solution)/shard_map/all_gather | solution.py:10
  7.3 166.4 %all-gather.4.cloned.1.call-start = ((), (), s32[]{:S(2)}) async-start(), calls=%async_computation.1 | async-start | bytes 9400320 | tf_op jit(solution)/shard_map/all_gather | solution.py:8
  8.0 199.3 %reduce-scatter.2.cloned.1.call-start = ((), (), s32[]{:S(2)}) async-start(), calls=%async_computation.2 | async-start | bytes 442368 | tf_op jit(solution)/shard_map/reduce_scatter | solution.py:15
Sparse Core Ops, SparseCore 0:
  9.5 51.9 all-gather.5
  63.6 110.0 all-gather.3
  185.6 21.6 reduce-scatter.1
where the time goes:
time: 214 us
  waiting for transfers between devices  176 us (82%)
  local copies, waits for them, and re-layouts  13.1 us (6%)
  between operations  13.1 us (6%)
  matrix products  11.8 us (6%)
    all_gather x1, waiting for transfers between devices, local(): slab = lax.all_gather(integrals, 'row', axis=0, tiled=True)  99.1 us
    all_gather x1, waiting for transfers between devices, local(): lax.all_gather(amplitudes, 'col', axis=1, tiled=True)  53.4 us
    reduce_scatter x1, waiting for transfers between devices, local(): lax.psum_scatter(0.5 * total, 'depth', scatter_dimension=0, tiled=True)  21.8 us
    dot_general x1, matrix products, local(): jnp.dot(lax.all_gather(amplitudes, 'col', axis=1, tiled=True), slab, prec...  11.8 us
    all_gather x1, local copies, waits for them, and re-layouts, local(): lax.all_gather(amplitudes, 'col', axis=1, tiled=True)  7.19 us
    unnamed x1, local copies, waits for them, and re-layouts  5.87 us
  transfers between devices with their start and end apart: 3, of which 3 were waited for; matrix products, arithmetic and copies ran while one was open for 6% of the time, Pallas kernels for 0%

commit v1 on v0

--- a/solution.py
+++ b/solution.py
@@ -5,7 +5,10 @@
 
 
 def local(amplitudes, integrals):
-    slab = lax.all_gather(integrals, "row", axis=0, tiled=True)
+    tmp = lax.axis_size("row")
+    latest = jnp.stack(tmp * [integrals], 0)
+    answer = lax.all_to_all(latest, axis_name="row", split_axis=0, concat_axis=0)
+    slab = jnp.concatenate(answer, 0)
     total = jnp.dot(
         lax.all_gather(amplitudes, "col", axis=1, tiled=True),
         slab,

time: 214 us -> 452 us (2.11)
  waiting for transfers between devices: 176 us -> 393 us
  starting transfers between devices: 0.08 us -> 15.9 us
  local copies, waits for them, and re-layouts: 13.1 us -> 18.1 us
    all_to_all x0 -> x1, waiting for transfers between devices: none -> 317 us  [local(): lax.all_to_all(latest, axis_name='row', split_axis=0, concat_axis=0)]
    all_gather x1 -> x0, waiting for transfers between devices: 99.1 us -> none  [local(): slab = lax.all_gather(integrals, 'row', axis=0, tiled=True)]
    all_to_all x0 -> x1, starting transfers between devices: none -> 15.8 us  [local(): lax.all_to_all(latest, axis_name='row', split_axis=0, concat_axis=0)]
    another operation x0 -> x1, local copies, waits for them, and re-layouts: none -> 5.06 us  [local(): latest = jnp.stack(tmp * [integrals], 0)]
  transfers between devices with their start and end apart: 3 -> 3, of which waited for: 3 -> 3; matrix products, arithmetic and copies ran while one was open for 6% -> 3% of each run, Pallas kernels for 0% -> 0%
where the time goes in v1:
time: 452 us
  waiting for transfers between devices  393 us (87%)
  local copies, waits for them, and re-layouts  18.1 us (4%)
  starting transfers between devices  15.9 us (4%)
  between operations  13.4 us (3%)
  matrix products  11.8 us (3%)
    all_to_all x1, waiting for transfers between devices, local(): lax.all_to_all(latest, axis_name='row', split_axis=0, concat_axis=0)  317 us
    all_gather x1, waiting for transfers between devices, local(): lax.all_gather(amplitudes, 'col', axis=1, tiled=True)  50.3 us
    reduce_scatter x1, waiting for transfers between devices, local(): lax.psum_scatter(0.5 * total, 'depth', scatter_dimension=0, tiled=True)  24.6 us
    all_to_all x1, starting transfers between devices, local(): lax.all_to_all(latest, axis_name='row', split_axis=0, concat_axis=0)  15.8 us
    dot_general x1, matrix products, local(): jnp.dot(lax.all_gather(amplitudes, 'col', axis=1, tiled=True), slab, prec...  11.8 us
  transfers between devices with their start and end apart: 3, of which 3 were waited for; matrix products, arithmetic and copies ran while one was open for 3% of the time, Pallas kernels for 0%

profile of v1, /device:TPU:1, one launch (start us, length us, event | category | flops | bytes accessed | tf_op | source)
XLA Modules:
  0.0 451.9 jit_solution(7981550543094723309)
XLA Ops:
  6.5 5.1 %stack.2 = f32[16,360,360]{2,1,0:T(8,128)} broadcast(f32[360,360]{1,0:T(8,128)} %param.3), dimensions={1,2} | broadcast | bytes 8812800 | tf_op jit(solution)/shard_map/stack | solution.py:9
  11.6 15.8 %all-to-all-start = ((f32[16,360,360]{2,1,0:T(8,128)}), f32[16,360,360]{2,1,0:T(8,128)}, u32[]{:S(2)}, u32[]{:S(2)}) async-start(f32[16,360,360]{2,1,0:T(8,128)} %stack.2), calls=%async_computation | async-start | bytes 17694720 | tf_op jit(solution)/shard_map/all_to_all | solution.py:10
  27.4 0.0 all-gather.3.cloned.1.call-start
  27.4 0.7 all-gather.3.cloned.1.call-update
  28.1 0.0 reduce-scatter.2.cloned.1.call-start
  28.2 50.3 %all-gather.3.cloned.1.call-done = f32[16,360,192]{1,2,0:T(8,128)} async-done(((f32[1,360,192]{1,2,0:T(8,128)}), f32[16,360,192]{1,2,0:T(8,128)}) %all-gather.3.cloned.1.call-update) | async-done | bytes 4423696 | tf_op jit(solution)/shard_map/all_gather | solution.py:13
  78.5 7.2 %copy.4 = f32[16,360,192]{1,0,2:T(8,128)} copy(f32[16,360,192]{1,2,0:T(8,128)} %all-gather.3.cloned.1.call-done) | data formatting | bytes 8847360 | tf_op jit(solution)/shard_map/all_gather | solution.py:13
  85.7 5.8 %reshape.7 = f32[5760,192]{0,1:T(8,128)} reshape(f32[16,360,192]{1,0,2:T(8,128)} %copy.4) | data formatting | bytes 8847360
  91.5 317.1 %all-to-all-done = f32[16,360,360]{2,1,0:T(8,128)} async-done(((f32[16,360,360]{2,1,0:T(8,128)}), f32[16,360,360]{2,1,0:T(8,128)}, u32[]{:S(2)}, u32[]{:S(2)}) %all-to-all-start) | async-done | bytes 8294432 | tf_op jit(solution)/shard_map/all_to_all | solution.py:10
  408.6 11.8 %convolution_multiply_fusion = f32[192,360]{1,0:T(8,128)} fusion(f32[5760,192]{0,1:T(8,128)} %reshape.7, f32[5760,360]{1,0:T(8,128)} %bitcast.2), kind=kOutput, calls=%fused_computation | convolution fusion | flops 4777643520 | bytes 12994560 | tf_op jit(solution)/shard_map/dot_general | solution.py:12
  420.4 0.0 reduce-scatter.2.cloned.1.call-update
  420.5 24.6 %reduce-scatter.2.cloned.1.call-done = f32[96,360]{1,0:T(8,128)} async-done(((f32[192,360]{1,0:T(8,128)}), f32[96,360]{1,0:T(8,128)}) %reduce-scatter.2.cloned.1.call-update) | async-done | bytes 138256 | tf_op jit(solution)/shard_map/reduce_scatter | solution.py:18
Async XLA Ops:
  11.6 397.0 %all-to-all-start = ((f32[16,360,360]{2,1,0:T(8,128)}), f32[16,360,360]{2,1,0:T(8,128)}, u32[]{:S(2)}, u32[]{:S(2)}) async-start(f32[16,360,360]{2,1,0:T(8,128)} %stack.2), calls=%async_computation | async-start | bytes 17694720 | tf_op jit(solution)/shard_map/all_to_all | solution.py:10
  27.4 51.1 %all-gather.3.cloned.1.call-start = ((), (), s32[]{:S(2)}) async-start(), calls=%async_computation.3 | async-start | bytes 5013504 | tf_op jit(solution)/shard_map/all_gather | solution.py:13
  28.1 416.9 %reduce-scatter.2.cloned.1.call-start = ((), (), s32[]{:S(2)}) async-start(), calls=%async_computation.2 | async-start | bytes 442368 | tf_op jit(solution)/shard_map/reduce_scatter | solution.py:18
Sparse Core Ops, SparseCore 0:
  30.4 48.0 all-gather.2
  420.6 24.4 reduce-scatter.1
